TPU v7x, 32 devices: a whole 2x2x4 slice. The times are simulated.
32 devices in a mesh: tower: 8 (over z, x), plate: 4 (over y, core).
Axes of the slice: x: 2, y: 2, z: 4, core: 2. Of those that a mesh axis runs over, the one named last changes fastest.
Arguments:
- features: bfloat16 [8, 1024, 128], P('tower', 'plate'), may hold values from -6 to 6
- adjoint: bfloat16 [8, 1024, 128], P('tower', 'plate'), may hold values from -6 to 6
- positions: bfloat16 [3, 8, 1024], P(None, 'tower', 'plate'), may hold values from 0 to 1
- w_rbf: bfloat16 [16, 128], replicated, may hold values from -1.5 to 1.5
- b_rbf: float32 [128], replicated, may hold values from -1 to 1
- w_filter: bfloat16 [128, 128], replicated, may hold values from -0.5 to 0.5
- b_filter: float32 [128], replicated, may hold values from -1 to 1
- atom_counts: int32 [8, 4], P('tower', 'plate'), may hold values from 128 to 256, as said below
- tile_counts: int32 [8, 4], P('tower', 'plate'), may hold values from 1 to 56, as said below
- tower_tiles: int32 [8, 4, 56], P('tower', 'plate'), may hold values from 0 to 23
- plate_tiles: int32 [8, 4, 56], P('tower', 'plate'), may hold values from 0 to 31
- image_shifts: int32 [8, 4, 56], P('tower', 'plate'), may hold values from 0 to 8
Outputs:
- grad_features: float32 [8, 1024, 128], P('tower', 'plate')
- grad_positions: float32 [3, 8, 1024], P(None, 'tower', 'plate')
- grad_w_rbf: float32 [16, 128], replicated
- grad_b_rbf: float32 [128], replicated
- grad_w_filter: float32 [128, 128], replicated
- grad_b_filter: float32 [128], replicated
Inputs may be any that keep to these rules, and one draw needn't show every extreme that they name: `atom_counts`: 256 in at least one brick. `tile_counts`: 56 in at least one brick; entries past the count are unused. `tower_tiles`: tiles below 8 lie in the brick below, the next 8 in the brick itself, the rest in the brick above. `plate_tiles`: tile v lies in brick v // 8 of the same plate. `image_shifts`: shift c moves the receiver by c // 3 - 1 along x and c % 3 - 1 along y.
All inputs are finite; a program needn't handle non-finite values.
Results may differ from a plain program's by a relative error of at most 0.005.
Values may be sent and summed in bfloat16 or wider, within the bound.
No kernel may reach another device: no remote copies, remote signals or barrier semaphores. Data moves between devices by JAX's collectives and lax.ppermute only.
A program may use at most 64 MiB of HBM per device.

v0:
```python
import math
import jax
import jax.numpy as jnp
from jax import lax
from jax.sharding import PartitionSpec as P

TILE = 32
box_side = 1.0
brick_height = 1.0
cutoff_radius = 3.0
soften = 0.01
sharpness = 10.0
log_two = math.log(2.0)


def shifted(block, axis, distance):
    devices = range(lax.axis_size(axis))
    route = [((i - distance) % len(devices), i) for i in devices]
    return lax.ppermute(block, axis, route)


def shift_vector(shift_code, tower_tile, per_brick):
    step_z = tower_tile // per_brick - 1
    return jnp.stack(
        [
            (shift_code // 3 - 1).astype(jnp.float32) * box_side,
            (shift_code % 3 - 1).astype(jnp.float32) * box_side,
            step_z.astype(jnp.float32) * brick_height,
        ]
    )


def pair_tile(adj_rows, recv_pos, feat_rows, send_pos, shift_vec, w_rbf, b_rbf, w_filter, b_filter):
    size_recv = adj_rows.shape[0]
    size_send = feat_rows.shape[0]
    feat_width = adj_rows.shape[1]
    displace = recv_pos[:, :, None] + shift_vec[:, None, None] - send_pos[:, None, :]
    distance = jnp.sqrt(jnp.sum(displace * displace, axis=0) + soften).reshape(-1)
    nbasis = w_rbf.shape[0]
    centres = jnp.arange(nbasis, dtype=jnp.float32) * (cutoff_radius / (nbasis - 1))
    offsets = distance[None, :] - centres[:, None]
    basis = jnp.exp(-sharpness * offsets * offsets)
    basis_b = basis.astype(jnp.bfloat16)
    preact = (
        lax.dot_general(
            basis_b, w_rbf, (((0,), (0,)), ((), ())), preferred_element_type=jnp.float32
        )
        + b_rbf
    )
    softed = (jax.nn.softplus(preact) - log_two).astype(jnp.bfloat16)
    filter_raw = jnp.dot(softed, w_filter, preferred_element_type=jnp.float32) + b_filter
    inside = distance < cutoff_radius
    phase_arg = math.pi / cutoff_radius * distance
    envelope = jnp.where(inside, 0.5 * (jnp.cos(phase_arg) + 1.0), 0.0)
    slope = jnp.where(inside, -0.5 * (math.pi / cutoff_radius) * jnp.sin(phase_arg), 0.0)
    adj_wide = adj_rows.astype(jnp.float32)
    feat_wide = feat_rows.astype(jnp.float32)
    filtered = (filter_raw * envelope[:, None]).reshape(size_recv, size_send, feat_width)
    grad_rows = jnp.einsum("if,ijf->jf", adj_wide, filtered)
    adjoint_pair = (adj_wide[:, None, :] * feat_wide[None, :, :]).reshape(
        size_recv * size_send, feat_width
    )
    d_raw = adjoint_pair * envelope[:, None]
    d_raw_b = d_raw.astype(jnp.bfloat16)
    grad_bf = jnp.sum(d_raw, axis=0)
    grad_wf = lax.dot_general(
        softed, d_raw_b, (((0,), (0,)), ((), ())), preferred_element_type=jnp.float32
    )
    d_soft = lax.dot_general(
        d_raw_b, w_filter, (((1,), (1,)), ((), ())), preferred_element_type=jnp.float32
    )
    d_pre = d_soft * jax.nn.sigmoid(preact)
    d_pre_b = d_pre.astype(jnp.bfloat16)
    grad_br = jnp.sum(d_pre, axis=0)
    grad_wr = lax.dot_general(
        basis_b, d_pre_b, (((1,), (0,)), ((), ())), preferred_element_type=jnp.float32
    )
    d_basis = lax.dot_general(
        w_rbf, d_pre_b, (((1,), (1,)), ((), ())), preferred_element_type=jnp.float32
    )
    d_dist = jnp.sum(d_basis * basis * (-2.0 * sharpness) * offsets, axis=0)
    d_dist = d_dist + jnp.sum(adjoint_pair * filter_raw, axis=1) * slope
    radial = (d_dist / distance).reshape(size_recv, size_send)
    pull = displace * radial[None]
    return (
        grad_rows,
        jnp.sum(pull, axis=2),
        -jnp.sum(pull, axis=1),
        (grad_wr, grad_br, grad_wf, grad_bf),
    )


def add_into(array, piece, starts):
    current = lax.dynamic_slice(array, starts, piece.shape)
    return lax.dynamic_update_slice(array, current + piece, starts)


def add_weights(left, right):
    return jax.tree.map(lambda first_term, second_term: first_term + second_term, left, right)


def local(
    features,
    adjoint,
    positions,
    w_rbf,
    b_rbf,
    w_filter,
    b_filter,
    atom_counts,
    tile_counts,
    tower_tiles,
    plate_tiles,
    image_shifts,
):
    brick_atoms = features.shape[1]
    feat_width = features.shape[2]
    tile_size = TILE
    per_brick = brick_atoms // tile_size
    plate_count = lax.axis_size("plate")
    zero_i = jnp.int32(0)
    live_mask = jnp.arange(brick_atoms, dtype=jnp.int32) < atom_counts[0, 0]
    zero_b = jnp.zeros((), jnp.bfloat16)
    own_feat = jnp.where(live_mask[:, None], features[0], zero_b)
    own_adj = jnp.where(live_mask[:, None], adjoint[0], zero_b)
    own_pos = positions[:, 0, :]
    from_below = shifted((own_adj, own_pos), "tower", 1)
    from_above = shifted((own_adj, own_pos), "tower", -1)
    tower_adj = jnp.concatenate([from_below[0], own_adj, from_above[0]], axis=0)
    tower_pos_b = jnp.concatenate([from_below[1], own_pos, from_above[1]], axis=1)
    tower_pos = tower_pos_b.astype(jnp.float32)
    weight_zero = (
        jnp.zeros(w_rbf.shape, jnp.float32),
        jnp.zeros(b_rbf.shape, jnp.float32),
        jnp.zeros(w_filter.shape, jnp.float32),
        jnp.zeros(b_filter.shape, jnp.float32),
    )
    plate_feat, plate_pos_b = (
        lax.all_gather(own_feat, "plate", axis=0, tiled=True),
        lax.all_gather(own_pos, "plate", axis=1, tiled=True),
    )
    plate_pos = plate_pos_b.astype(jnp.float32)

    def visit_listed(entry, totals):
        acc_dh, acc_gp, acc_tower, acc_weights = totals
        tower_tile = tower_tiles[0, 0, entry]
        plate_tile = plate_tiles[0, 0, entry]
        recv_start = tower_tile * tile_size
        send_start = plate_tile * tile_size
        adj_rows = lax.dynamic_slice_in_dim(tower_adj, recv_start, tile_size, 0)
        recv_pos = lax.dynamic_slice_in_dim(tower_pos, recv_start, tile_size, 1)
        feat_rows = lax.dynamic_slice_in_dim(plate_feat, send_start, tile_size, 0)
        send_pos = lax.dynamic_slice_in_dim(plate_pos, send_start, tile_size, 1)
        shift_vec = shift_vector(image_shifts[0, 0, entry], tower_tile, per_brick)
        grad_rows, grad_recv, grad_send, grad_weights = pair_tile(
            adj_rows, recv_pos, feat_rows, send_pos, shift_vec, w_rbf, b_rbf, w_filter, b_filter
        )
        brick_index = plate_tile // per_brick
        local_start = plate_tile % per_brick * tile_size
        acc_dh = add_into(acc_dh, grad_rows[None], (brick_index, local_start, zero_i))
        acc_gp = add_into(acc_gp, grad_send[None], (brick_index, zero_i, local_start))
        acc_tower = add_into(acc_tower, grad_recv, (zero_i, recv_start))
        return (acc_dh, acc_gp, acc_tower, add_weights(acc_weights, grad_weights))

    initial = (
        jnp.zeros((plate_count, brick_atoms, feat_width), jnp.float32),
        jnp.zeros((plate_count, 3, brick_atoms), jnp.float32),
        jnp.zeros((3, 3 * brick_atoms), jnp.float32),
        weight_zero,
    )
    acc_dh, acc_gp, tower_grad, acc_weights = lax.fori_loop(
        0, tile_counts[0, 0], visit_listed, initial
    )
    home_dh, home_gp = (
        lax.psum_scatter(acc_dh, "plate", scatter_dimension=0, tiled=True),
        lax.psum_scatter(acc_gp, "plate", scatter_dimension=0, tiled=True),
    )
    plate_dh = home_dh[0]
    plate_gp = home_gp[0]
    back_down = shifted(tower_grad[:, :brick_atoms], "tower", -1)
    back_up = shifted(tower_grad[:, 2 * brick_atoms :], "tower", 1)
    total_pos = plate_gp + tower_grad[:, brick_atoms : 2 * brick_atoms] + back_down + back_up
    tile_total = tile_counts[0, 0].astype(jnp.float32)
    summed = lax.psum(
        (acc_weights[0], acc_weights[1], acc_weights[2], acc_weights[3], tile_total),
        ("tower", "plate"),
    )
    scale = lax.rsqrt(summed[4] * (tile_size * tile_size))
    grad_features = jnp.where(live_mask[:, None], plate_dh, 0.0)[None]
    grad_positions = total_pos.reshape(3, 1, brick_atoms)
    return (
        grad_features,
        grad_positions,
        summed[0] * scale,
        summed[1] * scale,
        summed[2] * scale,
        summed[3] * scale,
    )


def solution(mesh):
    in_specs = (
        P("tower", "plate", None),
        P("tower", "plate", None),
        P(None, "tower", "plate"),
        P(),
        P(),
        P(),
        P(),
        P("tower", "plate"),
        P("tower", "plate"),
        P("tower", "plate", None),
        P("tower", "plate", None),
        P("tower", "plate", None),
    )
    out_specs = (P("tower", "plate", None), P(None, "tower", "plate"), P(), P(), P(), P())
    return jax.shard_map(local, mesh=mesh, in_specs=in_specs, out_specs=out_specs, check_vma=False)
```

profile of v0, /device:TPU:1, one launch (start us, length us, event | category | flops | bytes accessed | tf_op | source)
XLA Modules:
  0.0 1107.9 jit_solution(14880807231153509916)
XLA Ops:
  8.7 1.0 bitcast_select_fusion
  9.7 2.1 collective-permute-start.2
  11.8 3.1 collective-permute-start.3
  14.9 4.2 collective-permute-start.1
  19.0 6.5 all-gather
  25.6 5.9 all_gather.7
  31.7 0.6 copy-done.6
  32.4 304.2 %while.25 = (s32[]{:T(128)}, f32[4,256,128]{2,1,0:T(8,128)S(1)}, f32[4,3,256]{2,1,0:T(4,128)S(1)}, f32[3,768]{1,0:T(4,128)S(1)}, f32[16,128]{1,0:T(8,128)S(1)}, ...) while((s32[]{:T(128)}, f32[4,256,128]{2,1,0:T(8,128)S(1)}, ...), condition=%wide.region_8.9_spmd, body=%wide.region_0.8_spmd.sunk | while | flops 118017312 | bytes 6281055 | solution.py:171
  36.2 0.6 fusion.71
  41.5 0.6 constant_dynamic-slice_fusion.10
  43.7 0.6 fusion.73
  53.2 0.6 fusion.71
  58.4 0.6 constant_dynamic-slice_fusion.10
  60.6 0.6 fusion.73
  70.0 0.6 fusion.71
  75.2 0.6 constant_dynamic-slice_fusion.10
  77.4 0.6 fusion.73
  86.9 0.6 fusion.71
  92.1 0.6 constant_dynamic-slice_fusion.10
  94.4 0.6 fusion.73
  103.8 0.6 fusion.71
  109.1 0.6 constant_dynamic-slice_fusion.10
  111.3 0.6 fusion.73
  120.6 0.6 fusion.71
  125.9 0.6 constant_dynamic-slice_fusion.10
  128.1 0.6 fusion.73
  137.6 0.6 fusion.71
  145.0 0.6 fusion.73
  154.5 0.6 fusion.71
  161.9 0.6 fusion.73
  171.3 0.6 fusion.71
  178.7 0.6 fusion.73
  188.2 0.6 fusion.71
  195.7 0.6 fusion.73
  205.1 0.6 fusion.71
  210.3 0.6 constant_dynamic-slice_fusion.10
  212.6 0.6 fusion.73
  222.0 0.6 fusion.71
  227.2 0.6 constant_dynamic-slice_fusion.10
  229.5 0.6 fusion.73
  238.8 0.6 fusion.71
  246.3 0.6 fusion.73
  255.6 0.6 fusion.71
  263.0 0.6 fusion.73
  272.4 0.6 fusion.71
  277.6 0.6 constant_dynamic-slice_fusion.10
  279.8 0.6 fusion.73
  289.3 0.6 fusion.71
  296.8 0.6 fusion.73
  306.1 0.6 fusion.71
  313.6 0.6 fusion.73
  322.9 0.6 fusion.71
  328.1 0.6 constant_dynamic-slice_fusion.10
  330.4 0.6 fusion.73
  336.7 0.6 copy-done.1
  338.0 0.6 copy-done.10
  339.2 678.0 %all-reduce.1 = (f32[16,128]{1,0:T(8,128)S(1)}, f32[]{:T(128)}, f32[128]{0:T(128)S(1)}, f32[128]{0:T(128)S(1)}) all-reduce(f32[16,128]{1,0:T(8,128)S(1)} %get-tuple-element.335, f32[]{:T(128)S(6)} %convert_element_type.74, f32[128]{0:T(128)S(1)} %get-tuple-element.336, ...), channel_id=1, replica_groups=mesh['tower'=8,'plate'=4] {'tower','plate'}, use_global_device_ids=true, to_apply=%region_11.12 | all-reduce | flops 2305 | bytes 18440 | tf_op jit(solution)/shard_map/psum | solution.py:184
  1018.0 1.9 collective-permute-start.4
  1020.5 0.6 broadcast_multiply_fusion.3
  1021.1 10.9 all-reduce
  1032.0 0.7 fusion.28
  1033.3 64.1 %all-reduce.4.cloned.1.call-done = f32[128,128]{1,0:T(8,128)} async-done(((f32[128,128]{1,0:T(8,128)}), f32[128,128]{1,0:T(8,128)}) %all-reduce.4.cloned.1.call-update) | async-done | bytes 65552 | tf_op jit(solution)/shard_map/psum | solution.py:184
  1097.3 1.5 broadcast_multiply_fusion.2
  1098.8 1.7 broadcast_select_fusion
  (541 shorter events, 76.6 us)
Async XLA Ops:
  8.0 1089.3 %all-reduce.4.cloned.1.call-start = ((), (), s32[]{:S(2)}) async-start(), calls=%async_computation.2 | async-start | bytes 131072 | tf_op jit(solution)/shard_map/psum | solution.py:184
  9.7 5.2 copy-start.5
  9.7 21.8 %collective-permute-start.2 = (bf16[256,128]{1,0:T(8,128)(2,1)S(1)}, bf16[256,128]{1,0:T(8,128)(2,1)S(1)}, u32[]{:S(2)}, u32[]{:S(2)}) collective-permute-start(bf16[256,128]{1,0:T(8,128)(2,1)S(1)} %get-tuple-element.416), channel_id=1, source_target_pairs={{28,0},{0,4},{4,8},{8,12},{12,16},{16,20},{20,24},{24,28},{29,1},{... | collective-permute-start | bytes 196616 | tf_op jit(solution)/shard_map/ppermute | solution.py:19
  11.8 19.7 %collective-permute-start.3 = (bf16[256,128]{1,0:T(8,128)(2,1)S(1)}, bf16[256,128]{1,0:T(8,128)(2,1)S(1)}, u32[]{:S(2)}, u32[]{:S(2)}) collective-permute-start(bf16[256,128]{1,0:T(8,128)(2,1)S(1)} %get-tuple-element.416), channel_id=1, source_target_pairs={{4,0},{8,4},{12,8},{16,12},{20,16},{24,20},{28,24},{0,28},{5,1},{9... | collective-permute-start | bytes 196616 | tf_op jit(solution)/shard_map/ppermute | solution.py:19
  14.9 16.6 %collective-permute-start = (bf16[3,256]{1,0:T(4,128)(2,1)S(1)}, bf16[3,256]{1,0:T(4,128)(2,1)S(1)}, u32[]{:S(2)}, u32[]{:S(2)}) collective-permute-start(bf16[3,256]{1,0:T(4,128)(2,1)S(1)} %bitcast.114), channel_id=1, source_target_pairs={{28,0},{0,4},{4,8},{8,12},{12,16},{16,20},{20,24},{24,28},{29,1},{... | collective-permute-start | bytes 4616 | tf_op jit(solution)/shard_map/ppermute | solution.py:19
  14.9 16.6 %collective-permute-start.1 = (bf16[3,256]{1,0:T(4,128)(2,1)S(1)}, bf16[3,256]{1,0:T(4,128)(2,1)S(1)}, u32[]{:S(2)}, u32[]{:S(2)}) collective-permute-start(bf16[3,256]{1,0:T(4,128)(2,1)S(1)} %bitcast.115), channel_id=1, source_target_pairs={{4,0},{8,4},{12,8},{16,12},{20,16},{24,20},{28,24},{0,28},{5,1},{9... | collective-permute-start | bytes 4616 | tf_op jit(solution)/shard_map/ppermute | solution.py:19
  31.6 0.8 copy-start.6
  31.6 0.7 copy-start.8
  31.6 0.7 copy-start.9
  31.6 0.7 copy-start.2
  31.7 0.7 copy-start.3
  31.7 0.7 copy-start.4
  31.7 0.7 copy-start.7
  336.6 0.6 copy-start.1
  336.6 681.3 %copy-start = (f32[4,256,128]{2,1,0:T(8,128)}, f32[4,256,128]{2,1,0:T(8,128)S(1)}, u32[]{:S(2)}) copy-start(f32[4,256,128]{2,1,0:T(8,128)S(1)} %get-tuple-element.332) | copy-start | bytes 1572868
  337.3 761.5 %reduce-scatter.2.cloned.1.call-start = ((), (), s32[]{:S(2)}) async-start(), calls=%async_computation.1 | async-start | bytes 655360 | tf_op jit(solution)/shard_map/reduce_scatter | solution.py:175
  338.0 0.7 copy-start.10
  1018.0 14.0 %collective-permute-start.4 = (f32[3,256]{1,0:T(4,128)S(1)}, f32[3,256]{1,0:T(4,128)S(1)}, u32[]{:S(2)}, u32[]{:S(2)}) collective-permute-start(f32[3,256]{1,0:T(4,128)S(1)} %get-tuple-element.413), channel_id=1, source_target_pairs={{4,0},{8,4},{12,8},{16,12},{20,16},{24,20},{28,24},{0,28},{5,1},{9... | collective-permute-start | bytes 9224 | tf_op jit(solution)/shard_map/ppermute | solution.py:19
  1019.9 12.1 %collective-permute-start.5 = (f32[3,256]{1,0:T(4,128)S(1)}, f32[3,256]{1,0:T(4,128)S(1)}, u32[]{:S(2)}, u32[]{:S(2)}) collective-permute-start(f32[3,256]{1,0:T(4,128)S(1)} %get-tuple-element.414), channel_id=1, source_target_pairs={{28,0},{0,4},{4,8},{8,12},{12,16},{16,20},{20,24},{24,28},{29,1},{... | collective-permute-start | bytes 9224 | tf_op jit(solution)/shard_map/ppermute | solution.py:19
Sparse Core Ops, SparseCore 0:
  337.4 759.8 all-reduce.3
Sparse Core Ops, SparseCore 1:
  1018.1 22.2 reduce-scatter.1
where the time goes:
time: 1120 us; the launch traced here: 1110 us
  blocking collectives  701 us (63%)
  loops' own time  202 us (18%)
  waiting for transfers between devices  64.1 us (6%)
  matrix products  39.7 us (4%)
  other arithmetic  37 us (3%)
  local copies, waits for them, and re-layouts  34.4 us (3%)
  between operations  17.7 us (2%)
  starting transfers between devices  11.4 us (1%)
    psum x1, blocking collectives, local(): lax.psum((acc_weights[0], acc_weights[1], acc_weights[2], acc_weights[3],...  678 us
    another operation x1, loops' own time, local(): lax.fori_loop(0, tile_counts[0, 0], visit_listed, initial)  202 us
    psum x1, waiting for transfers between devices, local(): lax.psum((acc_weights[0], acc_weights[1], acc_weights[2], acc_weights[3],...  64.1 us
  transfers between devices with their start and end apart: 8, of which 1 were waited for; matrix products, arithmetic and copies ran while one was open for 0% of the time, Pallas kernels for 0%

commit v1 on v0

--- a/solution.py
+++ b/solution.py
@@ -182,8 +182,10 @@
     total_pos = plate_gp + tower_grad[:, brick_atoms : 2 * brick_atoms] + back_down + back_up
     tile_total = tile_counts[0, 0].astype(jnp.float32)
     summed = lax.psum(
-        (acc_weights[0], acc_weights[1], acc_weights[2], acc_weights[3], tile_total),
-        ("tower", "plate"),
+        lax.psum(
+            (acc_weights[0], acc_weights[1], acc_weights[2], acc_weights[3], tile_total), "plate"
+        ),
+        "tower",
     )
     scale = lax.rsqrt(summed[4] * (tile_size * tile_size))
     grad_features = jnp.where(live_mask[:, None], plate_dh, 0.0)[None]

time: 1120 us -> 1120 us (level)
  waiting for transfers between devices: 64.1 us -> 728 us
  blocking collectives: 701 us -> 43.3 us
    psum x1, blocking collectives: 678 us -> 18.4 us  [local(): lax.psum(lax.psum((acc_weights[0], acc_weights[1], acc_weights[2], acc_we...]
    psum x1, waiting for transfers between devices: 64.1 us -> 669 us  [local(): lax.psum((acc_weights[0], acc_weights[1], acc_weights[2], acc_weights[3],...]
    psum x0 -> x1, waiting for transfers between devices: none -> 32.3 us  [local(): lax.psum(lax.psum((acc_weights[0], acc_weights[1], acc_weights[2], acc_we...]
    reduce_scatter x1, waiting for transfers between devices: 0.01 us -> 24.4 us  [local(): lax.psum_scatter(acc_dh, 'plate', scatter_dimension=0, tiled=True)]
  transfers between devices with their start and end apart: 8 -> 9, of which waited for: 1 -> 5; matrix products, arithmetic and copies ran while one was open for 0% -> 0% of each run, Pallas kernels for 0% -> 0%
where the time goes in v1:
time: 1120 us; the launch traced here: 1110 us
  waiting for transfers between devices  728 us (65%)
  loops' own time  202 us (18%)
  blocking collectives  43.3 us (4%)
  matrix products  39.8 us (4%)
  other arithmetic  37.1 us (3%)
  local copies, waits for them, and re-layouts  34.4 us (3%)
  between operations  16 us (1%)
    psum x1, waiting for transfers between devices, local(): lax.psum((acc_weights[0], acc_weights[1], acc_weights[2], acc_weights[3],...  669 us
    another operation x1, loops' own time, local(): lax.fori_loop(0, tile_counts[0, 0], visit_listed, initial)  202 us
    psum x1, waiting for transfers between devices, local(): lax.psum(lax.psum((acc_weights[0], acc_weights[1], acc_weights[2], acc_we...  32.3 us
    reduce_scatter x1, waiting for transfers between devices, local(): lax.psum_scatter(acc_dh, 'plate', scatter_dimension=0, tiled=True)  24.4 us
  transfers between devices with their start and end apart: 9, of which 5 were waited for; matrix products, arithmetic and copies ran while one was open for 0% of the time, Pallas kernels for 0%

profile of v1, /device:TPU:1, one launch (start us, length us, event | category | flops | bytes accessed | tf_op | source)
XLA Modules:
  0.0 1111.9 jit_solution(10729105198202971981)
XLA Ops:
  7.9 1.0 bitcast_select_fusion
  8.9 2.1 collective-permute-start.2
  10.9 3.1 collective-permute-start.3
  14.1 4.2 collective-permute-start.1
  18.2 6.5 all-gather
  24.7 5.9 all_gather.7
  30.9 0.6 copy-done.6
  31.5 304.3 %while.25 = (s32[]{:T(128)}, f32[4,256,128]{2,1,0:T(8,128)S(1)}, f32[4,3,256]{2,1,0:T(4,128)S(1)}, f32[3,768]{1,0:T(4,128)S(1)}, f32[16,128]{1,0:T(8,128)S(1)}, ...) while((s32[]{:T(128)}, f32[4,256,128]{2,1,0:T(8,128)S(1)}, ...), condition=%wide.region_8.9_spmd, body=%wide.region_0.8_spmd.sunk | while | flops 118017312 | bytes 6281055 | solution.py:171
  35.4 0.6 fusion.71
  42.9 0.6 fusion.73
  52.3 0.6 fusion.71
  57.5 0.6 constant_dynamic-slice_fusion.10
  59.8 0.6 fusion.73
  69.1 0.6 fusion.71
  74.4 0.6 constant_dynamic-slice_fusion.10
  76.6 0.6 fusion.73
  86.1 0.6 fusion.71
  91.3 0.6 constant_dynamic-slice_fusion.10
  93.5 0.6 fusion.73
  103.0 0.6 fusion.71
  108.2 0.6 constant_dynamic-slice_fusion.10
  110.5 0.6 fusion.73
  119.8 0.6 fusion.71
  127.3 0.6 fusion.73
  136.7 0.6 fusion.71
  142.0 0.6 constant_dynamic-slice_fusion.10
  144.2 0.6 fusion.73
  153.6 0.6 fusion.71
  161.1 0.6 fusion.73
  170.5 0.6 fusion.71
  175.7 0.6 constant_dynamic-slice_fusion.10
  177.9 0.6 fusion.73
  187.4 0.6 fusion.71
  192.6 0.6 constant_dynamic-slice_fusion.10
  194.8 0.6 fusion.73
  204.3 0.6 fusion.71
  211.8 0.6 fusion.73
  221.2 0.6 fusion.71
  228.7 0.6 fusion.73
  238.0 0.6 fusion.71
  245.5 0.6 fusion.73
  254.7 0.6 fusion.71
  262.2 0.6 fusion.73
  271.6 0.6 fusion.71
  279.0 0.6 fusion.73
  288.5 0.6 fusion.71
  296.0 0.6 fusion.73
  305.3 0.6 fusion.71
  312.8 0.6 fusion.73
  322.1 0.6 fusion.71
  329.6 0.6 fusion.73
  335.9 0.6 copy-done.1
  336.6 668.9 %all-reduce.6.cloned.1.call-done = f32[128,128]{1,0:T(8,128)} async-done(((f32[128,128]{1,0:T(8,128)}), f32[128,128]{1,0:T(8,128)}) %all-reduce.6.cloned.1.call-update) | async-done | bytes 65552 | tf_op jit(solution)/shard_map/psum | solution.py:185
  1006.2 0.6 copy-done.10
  1007.4 12.5 %all-reduce.2 = (f32[4,3,256]{2,1,0:T(4,128)S(1)}, f32[16,128]{1,0:T(8,128)S(1)}, f32[]{:T(128)}, f32[128]{0:T(128)S(1)}, f32[128]{0:T(128)S(1)}) all-reduce(f32[4,3,256]{2,1,0:T(4,128)S(1)} %get-tuple-element.333, f32[16,128]{1,0:T(8,128)S(1)} %get-tuple-element.335, ...), channel_id=4, replica_groups=mesh['tower'=8,'plate'=4] {'plate'}, use_global_device_ids=true, to_apply=%region_10.11.clone | all-reduce | flops 5377 | bytes 43016
  1019.9 18.4 %all-reduce.1 = (f32[16,128]{1,0:T(8,128)S(1)}, f32[]{:T(128)}, f32[128]{0:T(128)S(1)}, f32[128]{0:T(128)S(1)}) all-reduce(f32[16,128]{1,0:T(8,128)S(1)} %get-tuple-element.398, f32[]{:T(128)} %get-tuple-element.399, f32[128]{0:T(128)S(1)} %get-tuple-element.400, ...), channel_id=1, replica_groups=mesh['tower'=8,'plate'=4] {'tower'}, use_global_device_ids=true, to_apply=%region_12.13 | all-reduce | flops 2305 | bytes 18440 | tf_op jit(solution)/shard_map/psum | solution.py:184
  1039.1 1.5 collective-permute-start.5
  1040.6 0.6 broadcast_multiply_fusion.3
  1041.9 2.5 collective-permute-done.5
  1044.4 0.7 fusion.28
  1045.6 32.3 %all-reduce.8.cloned.1.call-done = f32[128,128]{1,0:T(8,128)} async-done(((f32[128,128]{1,0:T(8,128)}), f32[128,128]{1,0:T(8,128)}) %all-reduce.8.cloned.1.call-update) | async-done | bytes 65552 | tf_op jit(solution)/shard_map/psum | solution.py:184
  1077.9 1.5 broadcast_multiply_fusion.2
  1079.3 24.4 %reduce-scatter.2.cloned.1.call-done = f32[1,256,128]{2,1,0:T(8,128)} async-done(((f32[4,256,128]{2,1,0:T(8,128)}), f32[1,256,128]{2,1,0:T(8,128)}) %reduce-scatter.2.cloned.1.call-update) | async-done | bytes 131088 | tf_op jit(solution)/shard_map/reduce_scatter | solution.py:175
  1103.7 1.7 broadcast_select_fusion
  (544 shorter events, 78.7 us)
Async XLA Ops:
  7.2 998.3 %all-reduce.6.cloned.1.call-start = ((), (), s32[]{:S(2)}) async-start(), calls=%async_computation.2 | async-start | bytes 131072 | tf_op jit(solution)/shard_map/psum | solution.py:185
  8.8 5.2 copy-start.5
  8.9 21.8 %collective-permute-start.2 = (bf16[256,128]{1,0:T(8,128)(2,1)S(1)}, bf16[256,128]{1,0:T(8,128)(2,1)S(1)}, u32[]{:S(2)}, u32[]{:S(2)}) collective-permute-start(bf16[256,128]{1,0:T(8,128)(2,1)S(1)} %get-tuple-element.421), channel_id=1, source_target_pairs={{28,0},{0,4},{4,8},{8,12},{12,16},{16,20},{20,24},{24,28},{29,1},{... | collective-permute-start | bytes 196616 | tf_op jit(solution)/shard_map/ppermute | solution.py:19
  10.9 19.7 %collective-permute-start.3 = (bf16[256,128]{1,0:T(8,128)(2,1)S(1)}, bf16[256,128]{1,0:T(8,128)(2,1)S(1)}, u32[]{:S(2)}, u32[]{:S(2)}) collective-permute-start(bf16[256,128]{1,0:T(8,128)(2,1)S(1)} %get-tuple-element.421), channel_id=1, source_target_pairs={{4,0},{8,4},{12,8},{16,12},{20,16},{24,20},{28,24},{0,28},{5,1},{9... | collective-permute-start | bytes 196616 | tf_op jit(solution)/shard_map/ppermute | solution.py:19
  14.1 16.6 %collective-permute-start = (bf16[3,256]{1,0:T(4,128)(2,1)S(1)}, bf16[3,256]{1,0:T(4,128)(2,1)S(1)}, u32[]{:S(2)}, u32[]{:S(2)}) collective-permute-start(bf16[3,256]{1,0:T(4,128)(2,1)S(1)} %bitcast.114), channel_id=1, source_target_pairs={{28,0},{0,4},{4,8},{8,12},{12,16},{16,20},{20,24},{24,28},{29,1},{... | collective-permute-start | bytes 4616 | tf_op jit(solution)/shard_map/ppermute | solution.py:19
  14.1 16.6 %collective-permute-start.1 = (bf16[3,256]{1,0:T(4,128)(2,1)S(1)}, bf16[3,256]{1,0:T(4,128)(2,1)S(1)}, u32[]{:S(2)}, u32[]{:S(2)}) collective-permute-start(bf16[3,256]{1,0:T(4,128)(2,1)S(1)} %bitcast.115), channel_id=1, source_target_pairs={{4,0},{8,4},{12,8},{16,12},{20,16},{24,20},{28,24},{0,28},{5,1},{9... | collective-permute-start | bytes 4616 | tf_op jit(solution)/shard_map/ppermute | solution.py:19
  30.8 0.8 copy-start.6
  30.8 0.7 copy-start.8
  30.8 0.7 copy-start.9
  30.8 0.7 copy-start.2
  30.8 0.7 copy-start.3
  30.9 0.7 copy-start.4
  30.9 0.7 copy-start.7
  335.9 0.6 copy-start.1
  335.9 703.2 %copy-start = (f32[4,256,128]{2,1,0:T(8,128)}, f32[4,256,128]{2,1,0:T(8,128)S(1)}, u32[]{:S(2)}) copy-start(f32[4,256,128]{2,1,0:T(8,128)S(1)} %get-tuple-element.332) | copy-start | bytes 1572868
  336.5 741.4 %all-reduce.8.cloned.1.call-start = ((), (), s32[]{:S(2)}) async-start(), calls=%async_computation.3 | async-start | bytes 131072 | tf_op jit(solution)/shard_map/psum | solution.py:184
  1005.5 98.2 %reduce-scatter.2.cloned.1.call-start = ((), (), s32[]{:S(2)}) async-start(), calls=%async_computation.1 | async-start | bytes 655360 | tf_op jit(solution)/shard_map/reduce_scatter | solution.py:175
  1006.2 0.7 copy-start.10
  1039.1 2.8 collective-permute-start.4
  1039.1 5.2 collective-permute-start.5
Sparse Core Ops, SparseCore 0:
  336.6 668.7 all-reduce.5
  1008.9 68.9 all-reduce.7
  1080.4 23.2 reduce-scatter.1
